TPU v7x, 128 devices: a whole 4x4x4 slice. The times are simulated.
128 devices in a mesh: seq: 32 (over x, y, core), tp: 4 (over z).
Axes of the slice: x: 4, y: 4, z: 4, core: 2. Of those that a mesh axis runs over, the one named last changes fastest.
Arguments:
- states_in: bfloat16 [8192, 2048], P('seq'), may hold values from -7 to 7
- lengths: int32 [4], replicated, may hold values from 1 to 64, 128 in all
- attn_gain: float32 [2048], replicated, may hold values from 0.5 to 1.5
- w_query: bfloat16 [2048, 2048], P(None, 'tp'), may hold values from -0.125 to 0.125
- w_key: bfloat16 [2048, 2048], P(None, 'tp'), may hold values from -0.088388348 to 0.088388348
- w_value: bfloat16 [2048, 4096], P(None, 'tp'), may hold values from -0.125 to 0.125
- w_gate: bfloat16 [2048, 4096], P(None, 'tp'), may hold values from -0.125 to 0.125
- w_beta: bfloat16 [2048, 16], P(None, 'tp'), may hold values from -1 to 1
- w_alpha: bfloat16 [2048, 16], P(None, 'tp'), may hold values from -0.125 to 0.125
- decay_rate: float32 [16], P('tp'), may hold values from 4.8828125e-05 to 0.05
- decay_bias: float32 [16], P('tp'), may hold values from -2 to 1
- conv_query: float32 [4, 2048], P(None, 'tp'), may hold values from -3 to 3
- conv_key: float32 [4, 2048], P(None, 'tp'), may hold values from -3 to 3
- conv_value: float32 [4, 4096], P(None, 'tp'), may hold values from -4.5 to 4.5
- out_gain: float32 [256], replicated, may hold values from 0.5 to 1.5
- w_out: bfloat16 [4096, 2048], P('tp'), may hold values from -0.09375 to 0.09375
- final_gain: float32 [2048], replicated, may hold values from 0.5 to 1.5
- w_head: bfloat16 [2048, 32000], P(None, ('seq', 'tp')), may hold values from -0.41992188 to 0.41992188
Outputs:
- hidden: bfloat16 [8192, 2048], P('seq', 'tp')
- block_states: float32 [128, 16, 128, 256], P('seq', 'tp')
- max_logit: float32 [4], replicated
Inputs may be any that keep to these rules, and one draw needn't show every extreme that they name: Prompt lengths are counted in blocks of 64 tokens; they sum to 128 and the longest is 64.
All inputs are finite; a program needn't handle non-finite values.
Results may differ from a plain program's by a relative error of at most 0.0095.
Values may be sent and summed in bfloat16 or wider, within the bound.
No kernel may reach another device: no remote copies, remote signals or barrier semaphores. Data moves between devices by JAX's collectives and lax.ppermute only.
A program may use at most 128 MiB of HBM per device.

v0:
```python
import jax
import jax.numpy as jnp
from jax import lax
from jax.sharding import PartitionSpec as P

CONV = 4
BLOCK_LEN = 64
EPS = 1e-06
HIGH = lax.Precision.HIGHEST


def from_behind(value, axis, steps):
    count = lax.axis_size(axis)
    first, last = (max(0, -steps), min(count, count - steps))
    return lax.ppermute(value, axis, [(source, source + steps) for source in range(first, last)])


def rms_scale(values, gain):
    return values * lax.rsqrt(jnp.mean(values * values, axis=-1, keepdims=True) + EPS) * gain


def unit_rows(values):
    return values * lax.rsqrt(jnp.sum(values * values, axis=-1, keepdims=True) + EPS)


def request_start(positions, offsets, block_len):
    block_ids = positions // block_len
    hits = offsets[None, :] <= block_ids[:, None]
    return block_len * jnp.max(jnp.where(hits, offsets[None, :], 0), axis=1)


def short_conv(extended, positions, start_tok, weight):
    row_count = positions.shape[0]
    tap_count = weight.shape[0]
    running = jnp.zeros((row_count, extended.shape[1]), jnp.float32)
    for tap_index in range(tap_count):
        lag_steps = tap_count - 1 - tap_index
        shifted = extended[tap_index : tap_index + row_count].astype(jnp.float32)
        valid = (positions - lag_steps >= start_tok)[:, None]
        running = running + jnp.where(valid, shifted, 0.0) * weight[tap_index]
    return jax.nn.silu(running)


def block_step(carry_state, block_inputs):
    q_rows, k_rows, v_rows, beta_rows, log_cum, keep_flag = block_inputs
    carry_state = carry_state * keep_flag
    block_len = q_rows.shape[1]
    row_ids = lax.broadcasted_iota(jnp.int32, (block_len, block_len), 0)
    col_ids = lax.broadcasted_iota(jnp.int32, (block_len, block_len), 1)
    on_lower = (row_ids >= col_ids).astype(jnp.float32)
    off_lower = (row_ids > col_ids).astype(jnp.float32)
    log_gap = log_cum[:, :, None] - log_cum[:, None, :]
    decays = jnp.exp(jnp.where(row_ids >= col_ids, log_gap, 0.0)) * on_lower
    growth = jnp.exp(log_cum)
    key_gram = jnp.einsum("hid,hjd->hij", k_rows, k_rows, precision=HIGH)
    system_mat = (
        jnp.eye(block_len, dtype=jnp.float32)
        + beta_rows[:, :, None] * key_gram * decays * off_lower
    )
    carried = jnp.einsum("hid,hde->hie", k_rows, carry_state, precision=HIGH)
    right_side = beta_rows[:, :, None] * (v_rows - growth[:, :, None] * carried)
    pseudo_values = lax.linalg.triangular_solve(
        system_mat, right_side, left_side=True, lower=True, unit_diagonal=True
    )
    scores = jnp.einsum("hid,hjd->hij", q_rows, k_rows, precision=HIGH) * decays
    output = growth[:, :, None] * jnp.einsum("hid,hde->hie", q_rows, carry_state, precision=HIGH)
    output = output + jnp.einsum("hij,hje->hie", scores, pseudo_values, precision=HIGH)
    tail_decay = jnp.exp(log_cum[:, -1:] - log_cum)
    carry_state = jnp.exp(log_cum[:, -1])[:, None, None] * carry_state + jnp.einsum(
        "hjd,hje->hde", k_rows * tail_decay[:, :, None], pseudo_values, precision=HIGH
    )
    return (carry_state, (output, carry_state))


def to_blocks(values, block_count, head_count):
    return values.reshape(block_count, BLOCK_LEN, head_count, -1).transpose(0, 2, 1, 3)


def body(
    states_in,
    lengths,
    attn_gain,
    w_query,
    w_key,
    w_value,
    w_gate,
    w_beta,
    w_alpha,
    decay_rate,
    decay_bias,
    conv_query,
    conv_key,
    conv_value,
    out_gain,
    w_out,
    final_gain,
    w_head,
):
    tok_dev = states_in.shape[0]
    heads_dev = decay_rate.shape[0]
    key_dim = w_query.shape[1] // heads_dev
    value_dim = w_value.shape[1] // heads_dev
    blocks_dev = tok_dev // BLOCK_LEN
    piece_index = lax.axis_index("seq")
    x_float = states_in.astype(jnp.float32)
    normed = rms_scale(x_float, attn_gain).astype(jnp.bfloat16)
    pre_q = jnp.dot(normed, w_query, preferred_element_type=jnp.float32).astype(jnp.bfloat16)
    pre_k = jnp.dot(normed, w_key, preferred_element_type=jnp.float32).astype(jnp.bfloat16)
    pre_v = jnp.dot(normed, w_value, preferred_element_type=jnp.float32).astype(jnp.bfloat16)
    gate_raw = jnp.dot(normed, w_gate, preferred_element_type=jnp.float32)
    beta_all = jax.nn.sigmoid(jnp.dot(normed, w_beta, preferred_element_type=jnp.float32))
    log_decay = -decay_rate * jax.nn.softplus(
        jnp.dot(normed, w_alpha, preferred_element_type=jnp.float32) + decay_bias
    )
    ends = jnp.cumsum(lengths)
    offsets = ends - lengths
    positions = piece_index * tok_dev + jnp.arange(tok_dev, dtype=jnp.int32)
    start_tok = request_start(positions, offsets, BLOCK_LEN)
    local_pre = jnp.concatenate([pre_q, pre_k, pre_v], axis=1)
    prev_edge = from_behind(local_pre[tok_dev - (CONV - 1) :], "seq", 1)
    extended = jnp.concatenate([prev_edge, local_pre], axis=0)
    conv_weights = jnp.concatenate([conv_query, conv_key, conv_value], axis=1)
    conv_all = short_conv(extended, positions, start_tok, conv_weights)
    qk_width = heads_dev * key_dim
    q_heads = unit_rows(conv_all[:, :qk_width].reshape(tok_dev, heads_dev, key_dim)) * key_dim ** (
        -0.5
    )
    k_heads = unit_rows(conv_all[:, qk_width : 2 * qk_width].reshape(tok_dev, heads_dev, key_dim))
    q_blocks = to_blocks(q_heads, blocks_dev, heads_dev)
    k_blocks = to_blocks(k_heads, blocks_dev, heads_dev)
    v_blocks = to_blocks(conv_all[:, 2 * qk_width :], blocks_dev, heads_dev)
    v_augmented = jnp.concatenate(
        [jnp.zeros(v_blocks.shape[:3] + (key_dim,), jnp.float32), v_blocks], axis=3
    )
    beta_blocks = beta_all.reshape(blocks_dev, BLOCK_LEN, heads_dev).transpose(0, 2, 1)
    log_blocks = jnp.cumsum(
        log_decay.reshape(blocks_dev, BLOCK_LEN, heads_dev).transpose(0, 2, 1), axis=2
    )
    block_ids = piece_index * blocks_dev + jnp.arange(blocks_dev, dtype=jnp.int32)
    keep_flags = 1.0 - jnp.max((offsets[None, :] == block_ids[:, None]).astype(jnp.float32), axis=1)
    eye_heads = jnp.broadcast_to(jnp.eye(key_dim, dtype=jnp.float32), (heads_dev, key_dim, key_dim))
    initial = jnp.concatenate(
        [eye_heads, jnp.zeros((heads_dev, key_dim, value_dim), jnp.float32)], axis=2
    )
    final_aug, (out_aug, states_aug) = lax.scan(
        block_step, initial, (q_blocks, k_blocks, v_augmented, beta_blocks, log_blocks, keep_flags)
    )
    lin_map = final_aug[:, :, :key_dim]
    offset_state = final_aug[:, :, key_dim:]

    def relay_turn(turn_index, incoming):
        outgoing = jnp.einsum("hde,hef->hdf", lin_map, incoming, precision=HIGH) + offset_state
        return from_behind(outgoing, "seq", 1)

    incoming = lax.fori_loop(0, lax.axis_size("seq") - 1, relay_turn, jnp.zeros_like(offset_state))
    o_blocks = out_aug[..., key_dim:] + jnp.einsum(
        "bhcd,hde->bhce", out_aug[..., :key_dim], incoming, precision=HIGH
    )
    block_states = (
        jnp.einsum("bhde,hef->bhdf", states_aug[..., :key_dim], incoming, precision=HIGH)
        + states_aug[..., key_dim:]
    )
    o_tokens = o_blocks.transpose(0, 2, 1, 3).reshape(tok_dev, heads_dev, value_dim)
    gated = (
        rms_scale(o_tokens, out_gain) * jax.nn.silu(gate_raw.reshape(tok_dev, heads_dev, value_dim))
    ).astype(jnp.bfloat16)
    partial_out = jnp.dot(
        gated.reshape(tok_dev, heads_dev * value_dim), w_out, preferred_element_type=jnp.float32
    )
    model_width = x_float.shape[1]
    share_cols = model_width // lax.axis_size("tp")
    col_start = lax.axis_index("tp") * share_cols
    last_tok = ends * BLOCK_LEN - 1
    picker = (last_tok[:, None] == positions[None, :]).astype(jnp.bfloat16)
    summed = lax.psum(partial_out, "tp")
    hidden_full = (x_float + summed).astype(jnp.bfloat16)
    hidden = lax.dynamic_slice_in_dim(hidden_full, col_start, share_cols, 1)
    picked = jnp.dot(picker, hidden_full, preferred_element_type=jnp.float32)
    last_rows = lax.psum(picked.astype(jnp.bfloat16), "seq").astype(jnp.float32)
    final = rms_scale(last_rows, final_gain).astype(jnp.bfloat16)
    logits = jnp.dot(final, w_head, preferred_element_type=jnp.float32)
    max_logit = lax.pmax(jnp.max(logits, axis=1), ("seq", "tp"))
    return (hidden, block_states, max_logit)


def solution(mesh):
    return jax.shard_map(
        body,
        mesh=mesh,
        in_specs=(
            P("seq", None),
            P(),
            P(),
            P(None, "tp"),
            P(None, "tp"),
            P(None, "tp"),
            P(None, "tp"),
            P(None, "tp"),
            P(None, "tp"),
            P("tp"),
            P("tp"),
            P(None, "tp"),
            P(None, "tp"),
            P(None, "tp"),
            P(),
            P("tp", None),
            P(),
            P(None, ("seq", "tp")),
        ),
        out_specs=(P("seq", "tp"), P("seq", "tp", None, None), P()),
        check_vma=False,
    )
```

profile of v0, /device:TPU:1, one launch (start us, length us, event | category | flops | bytes accessed | tf_op | source)
XLA Modules:
  0.0 931.8 jit_solution(14299696759197903953)
XLA Ops:
  51.5 133.2 %while.24 = (s32[]{:T(128)}, f32[4,128,384]{2,1,0:T(8,128)S(1)}, f32[4,4,64,384]{3,2,0,1:T(8,128)}, f32[4,4,128,384]{3,2,1,0:T(8,128)}, f32[4,4,64]{2,1,0:T(4,12...) while((s32[]{:T(128)}, f32[4,128,384]{2,1,0:T(8,128)S(1)}, ...), condition=%wide.region_8.9_spmd, body=%wide.region_7.8_spmd.sunk | while | flops 656073024 | bytes 11045709 | solution.py:145
  54.5 20.4 %custom-call.8 = f32[4,1,64,64]{2,3,1,0:T(8,128)S(1)} custom-call(f32[4,1,64,64]{3,2,1,0:T(8,128)} %fusion.136), custom_call_target="InvertDiagBlocksLowerTriangular" | custom-call | tf_op jit(solution)/shard_map/while/body/eval_jaxpr/triangular_solve | solution.py:62
  87.8 20.4 %custom-call.8 = f32[4,1,64,64]{2,3,1,0:T(8,128)S(1)} custom-call(f32[4,1,64,64]{3,2,1,0:T(8,128)} %fusion.136), custom_call_target="InvertDiagBlocksLowerTriangular" | custom-call | tf_op jit(solution)/shard_map/while/body/eval_jaxpr/triangular_solve | solution.py:62
  121.1 20.4 %custom-call.8 = f32[4,1,64,64]{2,3,1,0:T(8,128)S(1)} custom-call(f32[4,1,64,64]{3,2,1,0:T(8,128)} %fusion.136), custom_call_target="InvertDiagBlocksLowerTriangular" | custom-call | tf_op jit(solution)/shard_map/while/body/eval_jaxpr/triangular_solve | solution.py:62
  154.4 20.4 %custom-call.8 = f32[4,1,64,64]{2,3,1,0:T(8,128)S(1)} custom-call(f32[4,1,64,64]{3,2,1,0:T(8,128)} %fusion.136), custom_call_target="InvertDiagBlocksLowerTriangular" | custom-call | tf_op jit(solution)/shard_map/while/body/eval_jaxpr/triangular_solve | solution.py:62
  185.6 428.0 %while.25 = (s32[]{:T(128)}, f32[4,128,256]{2,1,0:T(8,128)S(1)}, f32[4,128,128]{2,1,0:T(8,128)}, f32[4,128,256]{2,1,0:T(8,128)S(1)}, s32[]{:T(128)}) while((s32[]{:T(128)}, f32[4,128,256]{2,1,0:T(8,128)S(1)}, f32[4,128,128]{2,1,0:T(8,128)}, f32[4,128,256]{2,1,0:T(8,128)S(1)}, s32[]{:T(128)}) %tuple.75), condition=%wide.region_10.11_spmd, body=%wide.region_9.10_spmd.sunk | while | flops 201457664 | bytes 3932261 | solution.py:155
  189.9 6.4 collective-permute-done
  202.9 6.4 collective-permute-done
  215.9 6.4 collective-permute-done
  228.9 6.4 collective-permute-done
  241.9 6.4 collective-permute-done
  255.0 6.4 collective-permute-done
  268.0 6.4 collective-permute-done
  281.0 6.4 collective-permute-done
  294.0 6.4 collective-permute-done
  307.1 6.4 collective-permute-done
  320.1 6.4 collective-permute-done
  333.1 6.4 collective-permute-done
  346.1 6.4 collective-permute-done
  359.2 6.4 collective-permute-done
  372.2 6.4 collective-permute-done
  398.2 6.4 collective-permute-done
  440.7 6.4 collective-permute-done
  471.0 6.4 collective-permute-done
  516.4 6.4 collective-permute-done
  546.7 6.4 collective-permute-done
  576.9 6.4 collective-permute-done
  592.1 6.4 collective-permute-done
  620.6 8.3 fusion.47
  637.6 89.2 %all-reduce.4.cloned.1.call-done = f32[256,2048]{1,0:T(8,128)} async-done(((f32[256,2048]{1,0:T(8,128)}), f32[256,2048]{1,0:T(8,128)}) %all-reduce.4.cloned.1.call-update) | async-done | bytes 2097168 | tf_op jit(solution)/shard_map/psum | solution.py:175
  729.2 123.1 %psum.15 = bf16[4,2048]{1,0:T(4,128)(2,1)S(1)} all-reduce(bf16[4,2048]{1,0:T(4,128)(2,1)S(1)} %convolution_convert_fusion), channel_id=1, replica_groups=mesh['seq'=32,'tp'=4] {'seq'}, use_global_device_ids=true, to_apply=%region_13.14 | all-reduce | flops 8192 | bytes 32768 | tf_op jit(solution)/shard_map/psum | solution.py:179
  857.0 67.2 %pmax.7 = f32[4]{0:T(128)} all-reduce(f32[4]{0:T(128)S(1)} %convolution_reduce_fusion), channel_id=1, replica_groups=mesh['seq'=32,'tp'=4] {'seq','tp'}, use_global_device_ids=true, to_apply=%region_16.17 | all-reduce | flops 4 | bytes 32 | tf_op jit(solution)/shard_map/pmax | solution.py:182
  (295 shorter events, 405.9 us)
Async XLA Ops:
  7.2 719.6 %all-reduce.4.cloned.1.call-start = ((), (), s32[]{:S(2)}) async-start(), calls=%async_computation | async-start | bytes 4194304 | tf_op jit(solution)/shard_map/psum | solution.py:175
  15.9 12.0 %collective-permute-start.1 = (bf16[3,2048]{1,0:T(4,128)(2,1)S(1)}, bf16[3,2048]{1,0:T(4,128)(2,1)S(1)}, u32[]{:S(2)}, u32[]{:S(2)}) collective-permute-start(bf16[3,2048]{1,0:T(4,128)(2,1)S(1)} %slice.76), channel_id=1, source_target_pairs={{0,4},{4,8},{8,12},{12,16},{16,20},{20,24},{24,28},{28,32},{32,36}... | collective-permute-start | bytes 36872 | tf_op jit(solution)/shard_map/ppermute | solution.py:15
  198.6 10.7 %collective-permute-start = (f32[4,128,256]{2,1,0:T(8,128)}, f32[4,128,256]{2,1,0:T(8,128)S(1)}, u32[]{:S(2)}, u32[]{:S(2)}) collective-permute-start(f32[4,128,256]{2,1,0:T(8,128)} %convolution_add_fusion.5), channel_id=1, source_target_pairs={{0,4},{4,8},{8,12},{12,16},{16,20},{20,24},{24,28},{28,32},{32,36}... | collective-permute-start | bytes 1572872 | tf_op jit(solution)/shard_map/while/body/eval_jaxpr/ppermute | solution.py:15
  211.6 10.7 %collective-permute-start = (f32[4,128,256]{2,1,0:T(8,128)}, f32[4,128,256]{2,1,0:T(8,128)S(1)}, u32[]{:S(2)}, u32[]{:S(2)}) collective-permute-start(f32[4,128,256]{2,1,0:T(8,128)} %convolution_add_fusion.5), channel_id=1, source_target_pairs={{0,4},{4,8},{8,12},{12,16},{16,20},{20,24},{24,28},{28,32},{32,36}... | collective-permute-start | bytes 1572872 | tf_op jit(solution)/shard_map/while/body/eval_jaxpr/ppermute | solution.py:15
  224.6 10.7 %collective-permute-start = (f32[4,128,256]{2,1,0:T(8,128)}, f32[4,128,256]{2,1,0:T(8,128)S(1)}, u32[]{:S(2)}, u32[]{:S(2)}) collective-permute-start(f32[4,128,256]{2,1,0:T(8,128)} %convolution_add_fusion.5), channel_id=1, source_target_pairs={{0,4},{4,8},{8,12},{12,16},{16,20},{20,24},{24,28},{28,32},{32,36}... | collective-permute-start | bytes 1572872 | tf_op jit(solution)/shard_map/while/body/eval_jaxpr/ppermute | solution.py:15
  237.7 10.7 %collective-permute-start = (f32[4,128,256]{2,1,0:T(8,128)}, f32[4,128,256]{2,1,0:T(8,128)S(1)}, u32[]{:S(2)}, u32[]{:S(2)}) collective-permute-start(f32[4,128,256]{2,1,0:T(8,128)} %convolution_add_fusion.5), channel_id=1, source_target_pairs={{0,4},{4,8},{8,12},{12,16},{16,20},{20,24},{24,28},{28,32},{32,36}... | collective-permute-start | bytes 1572872 | tf_op jit(solution)/shard_map/while/body/eval_jaxpr/ppermute | solution.py:15
  250.7 10.7 %collective-permute-start = (f32[4,128,256]{2,1,0:T(8,128)}, f32[4,128,256]{2,1,0:T(8,128)S(1)}, u32[]{:S(2)}, u32[]{:S(2)}) collective-permute-start(f32[4,128,256]{2,1,0:T(8,128)} %convolution_add_fusion.5), channel_id=1, source_target_pairs={{0,4},{4,8},{8,12},{12,16},{16,20},{20,24},{24,28},{28,32},{32,36}... | collective-permute-start | bytes 1572872 | tf_op jit(solution)/shard_map/while/body/eval_jaxpr/ppermute | solution.py:15
  263.7 10.7 %collective-permute-start = (f32[4,128,256]{2,1,0:T(8,128)}, f32[4,128,256]{2,1,0:T(8,128)S(1)}, u32[]{:S(2)}, u32[]{:S(2)}) collective-permute-start(f32[4,128,256]{2,1,0:T(8,128)} %convolution_add_fusion.5), channel_id=1, source_target_pairs={{0,4},{4,8},{8,12},{12,16},{16,20},{20,24},{24,28},{28,32},{32,36}... | collective-permute-start | bytes 1572872 | tf_op jit(solution)/shard_map/while/body/eval_jaxpr/ppermute | solution.py:15
  276.7 10.7 %collective-permute-start = (f32[4,128,256]{2,1,0:T(8,128)}, f32[4,128,256]{2,1,0:T(8,128)S(1)}, u32[]{:S(2)}, u32[]{:S(2)}) collective-permute-start(f32[4,128,256]{2,1,0:T(8,128)} %convolution_add_fusion.5), channel_id=1, source_target_pairs={{0,4},{4,8},{8,12},{12,16},{16,20},{20,24},{24,28},{28,32},{32,36}... | collective-permute-start | bytes 1572872 | tf_op jit(solution)/shard_map/while/body/eval_jaxpr/ppermute | solution.py:15
  289.8 10.7 %collective-permute-start = (f32[4,128,256]{2,1,0:T(8,128)}, f32[4,128,256]{2,1,0:T(8,128)S(1)}, u32[]{:S(2)}, u32[]{:S(2)}) collective-permute-start(f32[4,128,256]{2,1,0:T(8,128)} %convolution_add_fusion.5), channel_id=1, source_target_pairs={{0,4},{4,8},{8,12},{12,16},{16,20},{20,24},{24,28},{28,32},{32,36}... | collective-permute-start | bytes 1572872 | tf_op jit(solution)/shard_map/while/body/eval_jaxpr/ppermute | solution.py:15
  302.8 10.7 %collective-permute-start = (f32[4,128,256]{2,1,0:T(8,128)}, f32[4,128,256]{2,1,0:T(8,128)S(1)}, u32[]{:S(2)}, u32[]{:S(2)}) collective-permute-start(f32[4,128,256]{2,1,0:T(8,128)} %convolution_add_fusion.5), channel_id=1, source_target_pairs={{0,4},{4,8},{8,12},{12,16},{16,20},{20,24},{24,28},{28,32},{32,36}... | collective-permute-start | bytes 1572872 | tf_op jit(solution)/shard_map/while/body/eval_jaxpr/ppermute | solution.py:15
  315.8 10.7 %collective-permute-start = (f32[4,128,256]{2,1,0:T(8,128)}, f32[4,128,256]{2,1,0:T(8,128)S(1)}, u32[]{:S(2)}, u32[]{:S(2)}) collective-permute-start(f32[4,128,256]{2,1,0:T(8,128)} %convolution_add_fusion.5), channel_id=1, source_target_pairs={{0,4},{4,8},{8,12},{12,16},{16,20},{20,24},{24,28},{28,32},{32,36}... | collective-permute-start | bytes 1572872 | tf_op jit(solution)/shard_map/while/body/eval_jaxpr/ppermute | solution.py:15
  328.8 10.7 %collective-permute-start = (f32[4,128,256]{2,1,0:T(8,128)}, f32[4,128,256]{2,1,0:T(8,128)S(1)}, u32[]{:S(2)}, u32[]{:S(2)}) collective-permute-start(f32[4,128,256]{2,1,0:T(8,128)} %convolution_add_fusion.5), channel_id=1, source_target_pairs={{0,4},{4,8},{8,12},{12,16},{16,20},{20,24},{24,28},{28,32},{32,36}... | collective-permute-start | bytes 1572872 | tf_op jit(solution)/shard_map/while/body/eval_jaxpr/ppermute | solution.py:15
  341.9 10.7 %collective-permute-start = (f32[4,128,256]{2,1,0:T(8,128)}, f32[4,128,256]{2,1,0:T(8,128)S(1)}, u32[]{:S(2)}, u32[]{:S(2)}) collective-permute-start(f32[4,128,256]{2,1,0:T(8,128)} %convolution_add_fusion.5), channel_id=1, source_target_pairs={{0,4},{4,8},{8,12},{12,16},{16,20},{20,24},{24,28},{28,32},{32,36}... | collective-permute-start | bytes 1572872 | tf_op jit(solution)/shard_map/while/body/eval_jaxpr/ppermute | solution.py:15
  354.9 10.7 %collective-permute-start = (f32[4,128,256]{2,1,0:T(8,128)}, f32[4,128,256]{2,1,0:T(8,128)S(1)}, u32[]{:S(2)}, u32[]{:S(2)}) collective-permute-start(f32[4,128,256]{2,1,0:T(8,128)} %convolution_add_fusion.5), channel_id=1, source_target_pairs={{0,4},{4,8},{8,12},{12,16},{16,20},{20,24},{24,28},{28,32},{32,36}... | collective-permute-start | bytes 1572872 | tf_op jit(solution)/shard_map/while/body/eval_jaxpr/ppermute | solution.py:15
  367.9 10.7 %collective-permute-start = (f32[4,128,256]{2,1,0:T(8,128)}, f32[4,128,256]{2,1,0:T(8,128)S(1)}, u32[]{:S(2)}, u32[]{:S(2)}) collective-permute-start(f32[4,128,256]{2,1,0:T(8,128)} %convolution_add_fusion.5), channel_id=1, source_target_pairs={{0,4},{4,8},{8,12},{12,16},{16,20},{20,24},{24,28},{28,32},{32,36}... | collective-permute-start | bytes 1572872 | tf_op jit(solution)/shard_map/while/body/eval_jaxpr/ppermute | solution.py:15
  380.9 10.7 %collective-permute-start = (f32[4,128,256]{2,1,0:T(8,128)}, f32[4,128,256]{2,1,0:T(8,128)S(1)}, u32[]{:S(2)}, u32[]{:S(2)}) collective-permute-start(f32[4,128,256]{2,1,0:T(8,128)} %convolution_add_fusion.5), channel_id=1, source_target_pairs={{0,4},{4,8},{8,12},{12,16},{16,20},{20,24},{24,28},{28,32},{32,36}... | collective-permute-start | bytes 1572872 | tf_op jit(solution)/shard_map/while/body/eval_jaxpr/ppermute | solution.py:15
  394.0 10.7 %collective-permute-start = (f32[4,128,256]{2,1,0:T(8,128)}, f32[4,128,256]{2,1,0:T(8,128)S(1)}, u32[]{:S(2)}, u32[]{:S(2)}) collective-permute-start(f32[4,128,256]{2,1,0:T(8,128)} %convolution_add_fusion.5), channel_id=1, source_target_pairs={{0,4},{4,8},{8,12},{12,16},{16,20},{20,24},{24,28},{28,32},{32,36}... | collective-permute-start | bytes 1572872 | tf_op jit(solution)/shard_map/while/body/eval_jaxpr/ppermute | solution.py:15
  407.0 10.7 %collective-permute-start = (f32[4,128,256]{2,1,0:T(8,128)}, f32[4,128,256]{2,1,0:T(8,128)S(1)}, u32[]{:S(2)}, u32[]{:S(2)}) collective-permute-start(f32[4,128,256]{2,1,0:T(8,128)} %convolution_add_fusion.5), channel_id=1, source_target_pairs={{0,4},{4,8},{8,12},{12,16},{16,20},{20,24},{24,28},{28,32},{32,36}... | collective-permute-start | bytes 1572872 | tf_op jit(solution)/shard_map/while/body/eval_jaxpr/ppermute | solution.py:15
  420.0 12.0 %collective-permute-start = (f32[4,128,256]{2,1,0:T(8,128)}, f32[4,128,256]{2,1,0:T(8,128)S(1)}, u32[]{:S(2)}, u32[]{:S(2)}) collective-permute-start(f32[4,128,256]{2,1,0:T(8,128)} %convolution_add_fusion.5), channel_id=1, source_target_pairs={{0,4},{4,8},{8,12},{12,16},{16,20},{20,24},{24,28},{28,32},{32,36}... | collective-permute-start | bytes 1572872 | tf_op jit(solution)/shard_map/while/body/eval_jaxpr/ppermute | solution.py:15
  434.4 12.8 %collective-permute-start = (f32[4,128,256]{2,1,0:T(8,128)}, f32[4,128,256]{2,1,0:T(8,128)S(1)}, u32[]{:S(2)}, u32[]{:S(2)}) collective-permute-start(f32[4,128,256]{2,1,0:T(8,128)} %convolution_add_fusion.5), channel_id=1, source_target_pairs={{0,4},{4,8},{8,12},{12,16},{16,20},{20,24},{24,28},{28,32},{32,36}... | collective-permute-start | bytes 1572872 | tf_op jit(solution)/shard_map/while/body/eval_jaxpr/ppermute | solution.py:15
  449.5 12.8 %collective-permute-start = (f32[4,128,256]{2,1,0:T(8,128)}, f32[4,128,256]{2,1,0:T(8,128)S(1)}, u32[]{:S(2)}, u32[]{:S(2)}) collective-permute-start(f32[4,128,256]{2,1,0:T(8,128)} %convolution_add_fusion.5), channel_id=1, source_target_pairs={{0,4},{4,8},{8,12},{12,16},{16,20},{20,24},{24,28},{28,32},{32,36}... | collective-permute-start | bytes 1572872 | tf_op jit(solution)/shard_map/while/body/eval_jaxpr/ppermute | solution.py:15
  464.6 12.8 %collective-permute-start = (f32[4,128,256]{2,1,0:T(8,128)}, f32[4,128,256]{2,1,0:T(8,128)S(1)}, u32[]{:S(2)}, u32[]{:S(2)}) collective-permute-start(f32[4,128,256]{2,1,0:T(8,128)} %convolution_add_fusion.5), channel_id=1, source_target_pairs={{0,4},{4,8},{8,12},{12,16},{16,20},{20,24},{24,28},{28,32},{32,36}... | collective-permute-start | bytes 1572872 | tf_op jit(solution)/shard_map/while/body/eval_jaxpr/ppermute | solution.py:15
  479.7 12.8 %collective-permute-start = (f32[4,128,256]{2,1,0:T(8,128)}, f32[4,128,256]{2,1,0:T(8,128)S(1)}, u32[]{:S(2)}, u32[]{:S(2)}) collective-permute-start(f32[4,128,256]{2,1,0:T(8,128)} %convolution_add_fusion.5), channel_id=1, source_target_pairs={{0,4},{4,8},{8,12},{12,16},{16,20},{20,24},{24,28},{28,32},{32,36}... | collective-permute-start | bytes 1572872 | tf_op jit(solution)/shard_map/while/body/eval_jaxpr/ppermute | solution.py:15
  494.9 12.8 %collective-permute-start = (f32[4,128,256]{2,1,0:T(8,128)}, f32[4,128,256]{2,1,0:T(8,128)S(1)}, u32[]{:S(2)}, u32[]{:S(2)}) collective-permute-start(f32[4,128,256]{2,1,0:T(8,128)} %convolution_add_fusion.5), channel_id=1, source_target_pairs={{0,4},{4,8},{8,12},{12,16},{16,20},{20,24},{24,28},{28,32},{32,36}... | collective-permute-start | bytes 1572872 | tf_op jit(solution)/shard_map/while/body/eval_jaxpr/ppermute | solution.py:15
  510.0 12.8 %collective-permute-start = (f32[4,128,256]{2,1,0:T(8,128)}, f32[4,128,256]{2,1,0:T(8,128)S(1)}, u32[]{:S(2)}, u32[]{:S(2)}) collective-permute-start(f32[4,128,256]{2,1,0:T(8,128)} %convolution_add_fusion.5), channel_id=1, source_target_pairs={{0,4},{4,8},{8,12},{12,16},{16,20},{20,24},{24,28},{28,32},{32,36}... | collective-permute-start | bytes 1572872 | tf_op jit(solution)/shard_map/while/body/eval_jaxpr/ppermute | solution.py:15
  525.1 12.8 %collective-permute-start = (f32[4,128,256]{2,1,0:T(8,128)}, f32[4,128,256]{2,1,0:T(8,128)S(1)}, u32[]{:S(2)}, u32[]{:S(2)}) collective-permute-start(f32[4,128,256]{2,1,0:T(8,128)} %convolution_add_fusion.5), channel_id=1, source_target_pairs={{0,4},{4,8},{8,12},{12,16},{16,20},{20,24},{24,28},{28,32},{32,36}... | collective-permute-start | bytes 1572872 | tf_op jit(solution)/shard_map/while/body/eval_jaxpr/ppermute | solution.py:15
  540.3 12.8 %collective-permute-start = (f32[4,128,256]{2,1,0:T(8,128)}, f32[4,128,256]{2,1,0:T(8,128)S(1)}, u32[]{:S(2)}, u32[]{:S(2)}) collective-permute-start(f32[4,128,256]{2,1,0:T(8,128)} %convolution_add_fusion.5), channel_id=1, source_target_pairs={{0,4},{4,8},{8,12},{12,16},{16,20},{20,24},{24,28},{28,32},{32,36}... | collective-permute-start | bytes 1572872 | tf_op jit(solution)/shard_map/while/body/eval_jaxpr/ppermute | solution.py:15
  555.4 12.8 %collective-permute-start = (f32[4,128,256]{2,1,0:T(8,128)}, f32[4,128,256]{2,1,0:T(8,128)S(1)}, u32[]{:S(2)}, u32[]{:S(2)}) collective-permute-start(f32[4,128,256]{2,1,0:T(8,128)} %convolution_add_fusion.5), channel_id=1, source_target_pairs={{0,4},{4,8},{8,12},{12,16},{16,20},{20,24},{24,28},{28,32},{32,36}... | collective-permute-start | bytes 1572872 | tf_op jit(solution)/shard_map/while/body/eval_jaxpr/ppermute | solution.py:15
  570.5 12.8 %collective-permute-start = (f32[4,128,256]{2,1,0:T(8,128)}, f32[4,128,256]{2,1,0:T(8,128)S(1)}, u32[]{:S(2)}, u32[]{:S(2)}) collective-permute-start(f32[4,128,256]{2,1,0:T(8,128)} %convolution_add_fusion.5), channel_id=1, source_target_pairs={{0,4},{4,8},{8,12},{12,16},{16,20},{20,24},{24,28},{28,32},{32,36}... | collective-permute-start | bytes 1572872 | tf_op jit(solution)/shard_map/while/body/eval_jaxpr/ppermute | solution.py:15
  585.7 12.8 %collective-permute-start = (f32[4,128,256]{2,1,0:T(8,128)}, f32[4,128,256]{2,1,0:T(8,128)S(1)}, u32[]{:S(2)}, u32[]{:S(2)}) collective-permute-start(f32[4,128,256]{2,1,0:T(8,128)} %convolution_add_fusion.5), channel_id=1, source_target_pairs={{0,4},{4,8},{8,12},{12,16},{16,20},{20,24},{24,28},{28,32},{32,36}... | collective-permute-start | bytes 1572872 | tf_op jit(solution)/shard_map/while/body/eval_jaxpr/ppermute | solution.py:15
  600.8 12.8 %collective-permute-start = (f32[4,128,256]{2,1,0:T(8,128)}, f32[4,128,256]{2,1,0:T(8,128)S(1)}, u32[]{:S(2)}, u32[]{:S(2)}) collective-permute-start(f32[4,128,256]{2,1,0:T(8,128)} %convolution_add_fusion.5), channel_id=1, source_target_pairs={{0,4},{4,8},{8,12},{12,16},{16,20},{20,24},{24,28},{28,32},{32,36}... | collective-permute-start | bytes 1572872 | tf_op jit(solution)/shard_map/while/body/eval_jaxpr/ppermute | solution.py:15
  (41 other events, 462.0 us)
Sparse Core Ops, SparseCore 0:
  629.0 97.7 all-reduce.3
where the time goes:
time: 935 us; the launch traced here: 932 us
  waiting for transfers between devices  288 us (31%)
  blocking collectives  190 us (20%)
  starting transfers between devices  161 us (17%)
  matrix products  136 us (15%)
  other arithmetic  100 us (11%)
  local copies, waits for them, and re-layouts  40.7 us (4%)
  between operations  14.5 us (2%)
    ppermute x32, waiting for transfers between devices, from_behind(): lax.ppermute(value, axis, [(source, source + steps) for source in range(f...  199 us
    ppermute x32, starting transfers between devices, from_behind(): lax.ppermute(value, axis, [(source, source + steps) for source in range(f...  161 us
    psum x1, blocking collectives, body(): last_rows = lax.psum(picked.astype(jnp.bfloat16), 'seq').astype(jnp.float32)  123 us
    psum x1, waiting for transfers between devices, body(): summed = lax.psum(partial_out, 'tp')  89.2 us
    another operation x12, other arithmetic, block_step(): lax.linalg.triangular_solve(system_mat, right_side, left_side=True, lower...  81.6 us
    dot_general x31, matrix products, relay_turn(): jnp.einsum('hde,hef->hdf', lin_map, incoming, precision=HIGH) + offset_state  72.1 us
    pmax x1, blocking collectives, body(): max_logit = lax.pmax(jnp.max(logits, axis=1), ('seq', 'tp'))  67.2 us
  transfers between devices with their start and end apart: 33, of which 32 were waited for; matrix products, arithmetic and copies ran while one was open for 2% of the time, Pallas kernels for 0%

commit v1 on v0

--- a/solution.py
+++ b/solution.py
@@ -1,3 +1,4 @@
+import functools
 import jax
 import jax.numpy as jnp
 from jax import lax
@@ -7,6 +8,19 @@
 BLOCK_LEN = 64
 EPS = 1e-06
 HIGH = lax.Precision.HIGHEST
+
+
+def return_all_column_for(chunk, which_axis):
+    n_slots = lax.axis_size(which_axis)
+    a_now = lambda k_now: [(b, b ^ k_now) for b in range(n_slots)]
+    extra = chunk
+    for j in range(n_slots.bit_length() - 1):
+        taken_in = lax.ppermute(extra, which_axis, a_now(1 << j))
+        extra = extra + taken_in
+    return extra
+
+
+trace_lanes = functools.partial(return_all_column_for, which_axis="tp")
 
 
 def from_behind(value, axis, steps):
@@ -172,7 +186,7 @@
     col_start = lax.axis_index("tp") * share_cols
     last_tok = ends * BLOCK_LEN - 1
     picker = (last_tok[:, None] == positions[None, :]).astype(jnp.bfloat16)
-    summed = lax.psum(partial_out, "tp")
+    summed = trace_lanes(partial_out)
     hidden_full = (x_float + summed).astype(jnp.bfloat16)
     hidden = lax.dynamic_slice_in_dim(hidden_full, col_start, share_cols, 1)
     picked = jnp.dot(picker, hidden_full, preferred_element_type=jnp.float32)

time: 935 us -> 932 us (level)
  waiting for transfers between devices: 288 us -> 267 us
  blocking collectives: 190 us -> 210 us
  between operations: 14.5 us -> 1.13 us
    psum x1 -> x0, waiting for transfers between devices: 89.2 us -> none  [body(): summed = lax.psum(partial_out, 'tp')]
    ppermute x0 -> x2, waiting for transfers between devices: none -> 68.3 us  [return_all_column_for(): taken_in = lax.ppermute(extra, which_axis, a_now(1 << j))]
    psum x1, blocking collectives: 123 us -> 143 us  [body(): last_rows = lax.psum(picked.astype(jnp.bfloat16), 'seq').astype(jnp.float32)]
  transfers between devices with their start and end apart: 33 -> 34, of which waited for: 32 -> 33; matrix products, arithmetic and copies ran while one was open for 2% -> 2% of each run, Pallas kernels for 0% -> 0%
where the time goes in v1:
time: 932 us; the launch traced here: 929 us
  waiting for transfers between devices  267 us (29%)
  blocking collectives  210 us (23%)
  starting transfers between devices  169 us (18%)
  matrix products  136 us (15%)
  other arithmetic  104 us (11%)
  local copies, waits for them, and re-layouts  40.9 us (4%)
    ppermute x32, waiting for transfers between devices, from_behind(): lax.ppermute(value, axis, [(source, source + steps) for source in range(f...  199 us
    ppermute x32, starting transfers between devices, from_behind(): lax.ppermute(value, axis, [(source, source + steps) for source in range(f...  161 us
    psum x1, blocking collectives, body(): last_rows = lax.psum(picked.astype(jnp.bfloat16), 'seq').astype(jnp.float32)  143 us
    another operation x12, other arithmetic, block_step(): lax.linalg.triangular_solve(system_mat, right_side, left_side=True, lower...  81.6 us
    dot_general x31, matrix products, relay_turn(): jnp.einsum('hde,hef->hdf', lin_map, incoming, precision=HIGH) + offset_state  72.2 us
    ppermute x2, waiting for transfers between devices, return_all_column_for(): taken_in = lax.ppermute(extra, which_axis, a_now(1 << j))  68.3 us
    pmax x1, blocking collectives, body(): max_logit = lax.pmax(jnp.max(logits, axis=1), ('seq', 'tp'))  67 us
  transfers between devices with their start and end apart: 34, of which 33 were waited for; matrix products, arithmetic and copies ran while one was open for 2% of the time, Pallas kernels for 0%

profile of v1, /device:TPU:1, one launch (start us, length us, event | category | flops | bytes accessed | tf_op | source)
XLA Modules:
  0.0 928.7 jit_solution(3219947116932464309)
XLA Ops:
  44.9 133.5 %while.24 = (s32[]{:T(128)}, f32[4,128,384]{2,1,0:T(8,128)S(1)}, f32[4,4,64,384]{3,2,0,1:T(8,128)}, f32[4,4,128,384]{3,2,1,0:T(8,128)}, f32[4,4,64]{2,1,0:T(4,12...) while((s32[]{:T(128)}, f32[4,128,384]{2,1,0:T(8,128)S(1)}, ...), condition=%wide.region_8.9_spmd, body=%wide.region_7.8_spmd.sunk | while | flops 656073024 | bytes 11045709 | solution.py:159
  47.9 20.4 %custom-call.8 = f32[4,1,64,64]{2,3,1,0:T(8,128)S(1)} custom-call(f32[4,1,64,64]{3,2,1,0:T(8,128)} %fusion.136), custom_call_target="InvertDiagBlocksLowerTriangular" | custom-call | tf_op jit(solution)/shard_map/while/body/eval_jaxpr/triangular_solve | solution.py:76
  81.3 20.4 %custom-call.8 = f32[4,1,64,64]{2,3,1,0:T(8,128)S(1)} custom-call(f32[4,1,64,64]{3,2,1,0:T(8,128)} %fusion.136), custom_call_target="InvertDiagBlocksLowerTriangular" | custom-call | tf_op jit(solution)/shard_map/while/body/eval_jaxpr/triangular_solve | solution.py:76
  114.6 20.4 %custom-call.8 = f32[4,1,64,64]{2,3,1,0:T(8,128)S(1)} custom-call(f32[4,1,64,64]{3,2,1,0:T(8,128)} %fusion.136), custom_call_target="InvertDiagBlocksLowerTriangular" | custom-call | tf_op jit(solution)/shard_map/while/body/eval_jaxpr/triangular_solve | solution.py:76
  148.0 20.4 %custom-call.8 = f32[4,1,64,64]{2,3,1,0:T(8,128)S(1)} custom-call(f32[4,1,64,64]{3,2,1,0:T(8,128)} %fusion.136), custom_call_target="InvertDiagBlocksLowerTriangular" | custom-call | tf_op jit(solution)/shard_map/while/body/eval_jaxpr/triangular_solve | solution.py:76
  179.2 428.2 %while.25 = (s32[]{:T(128)}, f32[4,128,256]{2,1,0:T(8,128)S(1)}, f32[4,128,128]{2,1,0:T(8,128)}, f32[4,128,256]{2,1,0:T(8,128)S(1)}, s32[]{:T(128)}) while((s32[]{:T(128)}, f32[4,128,256]{2,1,0:T(8,128)S(1)}, f32[4,128,128]{2,1,0:T(8,128)}, f32[4,128,256]{2,1,0:T(8,128)S(1)}, s32[]{:T(128)}) %tuple.75), condition=%wide.region_10.11_spmd, body=%wide.region_9.10_spmd.sunk | while | flops 201457664 | bytes 3932261 | solution.py:169
  183.5 6.4 collective-permute-done
  196.5 6.4 collective-permute-done
  209.5 6.4 collective-permute-done
  222.6 6.4 collective-permute-done
  235.6 6.4 collective-permute-done
  248.6 6.4 collective-permute-done
  261.6 6.4 collective-permute-done
  274.7 6.4 collective-permute-done
  287.7 6.4 collective-permute-done
  300.7 6.4 collective-permute-done
  313.7 6.4 collective-permute-done
  326.8 6.4 collective-permute-done
  339.8 6.4 collective-permute-done
  352.8 6.4 collective-permute-done
  365.9 6.4 collective-permute-done
  378.9 6.4 collective-permute-done
  391.9 6.4 collective-permute-done
  479.9 6.4 collective-permute-done
  495.0 6.4 collective-permute-done
  510.1 6.4 collective-permute-done
  525.3 6.4 collective-permute-done
  614.3 8.3 fusion.47
  624.2 37.7 %collective-permute-done.2 = f32[256,2048]{1,0:T(8,128)S(1)} collective-permute-done((f32[256,2048]{1,0:T(8,128)}, f32[256,2048]{1,0:T(8,128)S(1)}, u32[]{:S(2)}, u32[]{:S(2)}) %collective-permute-start.2) | collective-permute-done | bytes 2097184 | tf_op jit(solution)/shard_map/ppermute | solution.py:18
  679.9 30.5 %collective-permute-done.3 = f32[256,2048]{1,0:T(8,128)} collective-permute-done((f32[256,2048]{1,0:T(8,128)}, f32[256,2048]{1,0:T(8,128)}, u32[]{:S(2)}, u32[]{:S(2)}) %collective-permute-start.3) | collective-permute-done | bytes 2097184 | tf_op jit(solution)/shard_map/ppermute | solution.py:18
  713.5 142.9 %psum.7 = bf16[4,2048]{1,0:T(4,128)(2,1)S(1)} all-reduce(bf16[4,2048]{1,0:T(4,128)(2,1)S(1)} %convolution_convert_fusion), channel_id=1, replica_groups=mesh['seq'=32,'tp'=4] {'seq'}, use_global_device_ids=true, to_apply=%region_12.13 | all-reduce | flops 8192 | bytes 32768 | tf_op jit(solution)/shard_map/psum | solution.py:193
  861.0 67.0 %pmax.7 = f32[4]{0:T(128)} all-reduce(f32[4]{0:T(128)S(1)} %convolution_reduce_fusion), channel_id=1, replica_groups=mesh['seq'=32,'tp'=4] {'seq','tp'}, use_global_device_ids=true, to_apply=%region_15.16 | all-reduce | flops 4 | bytes 32 | tf_op jit(solution)/shard_map/pmax | solution.py:196
  (299 shorter events, 424.2 us)
Async XLA Ops:
  9.4 12.0 %collective-permute-start.1 = (bf16[3,2048]{1,0:T(4,128)(2,1)S(1)}, bf16[3,2048]{1,0:T(4,128)(2,1)S(1)}, u32[]{:S(2)}, u32[]{:S(2)}) collective-permute-start(bf16[3,2048]{1,0:T(4,128)(2,1)S(1)} %slice.76), channel_id=1, source_target_pairs={{0,4},{4,8},{8,12},{12,16},{16,20},{20,24},{24,28},{28,32},{32,36}... | collective-permute-start | bytes 36872 | tf_op jit(solution)/shard_map/ppermute | solution.py:29
  192.2 10.7 %collective-permute-start = (f32[4,128,256]{2,1,0:T(8,128)}, f32[4,128,256]{2,1,0:T(8,128)S(1)}, u32[]{:S(2)}, u32[]{:S(2)}) collective-permute-start(f32[4,128,256]{2,1,0:T(8,128)} %convolution_add_fusion.5), channel_id=1, source_target_pairs={{0,4},{4,8},{8,12},{12,16},{16,20},{20,24},{24,28},{28,32},{32,36}... | collective-permute-start | bytes 1572872 | tf_op jit(solution)/shard_map/while/body/eval_jaxpr/ppermute | solution.py:29
  205.2 10.7 %collective-permute-start = (f32[4,128,256]{2,1,0:T(8,128)}, f32[4,128,256]{2,1,0:T(8,128)S(1)}, u32[]{:S(2)}, u32[]{:S(2)}) collective-permute-start(f32[4,128,256]{2,1,0:T(8,128)} %convolution_add_fusion.5), channel_id=1, source_target_pairs={{0,4},{4,8},{8,12},{12,16},{16,20},{20,24},{24,28},{28,32},{32,36}... | collective-permute-start | bytes 1572872 | tf_op jit(solution)/shard_map/while/body/eval_jaxpr/ppermute | solution.py:29
  218.3 10.7 %collective-permute-start = (f32[4,128,256]{2,1,0:T(8,128)}, f32[4,128,256]{2,1,0:T(8,128)S(1)}, u32[]{:S(2)}, u32[]{:S(2)}) collective-permute-start(f32[4,128,256]{2,1,0:T(8,128)} %convolution_add_fusion.5), channel_id=1, source_target_pairs={{0,4},{4,8},{8,12},{12,16},{16,20},{20,24},{24,28},{28,32},{32,36}... | collective-permute-start | bytes 1572872 | tf_op jit(solution)/shard_map/while/body/eval_jaxpr/ppermute | solution.py:29
  231.3 10.7 %collective-permute-start = (f32[4,128,256]{2,1,0:T(8,128)}, f32[4,128,256]{2,1,0:T(8,128)S(1)}, u32[]{:S(2)}, u32[]{:S(2)}) collective-permute-start(f32[4,128,256]{2,1,0:T(8,128)} %convolution_add_fusion.5), channel_id=1, source_target_pairs={{0,4},{4,8},{8,12},{12,16},{16,20},{20,24},{24,28},{28,32},{32,36}... | collective-permute-start | bytes 1572872 | tf_op jit(solution)/shard_map/while/body/eval_jaxpr/ppermute | solution.py:29
  244.3 10.7 %collective-permute-start = (f32[4,128,256]{2,1,0:T(8,128)}, f32[4,128,256]{2,1,0:T(8,128)S(1)}, u32[]{:S(2)}, u32[]{:S(2)}) collective-permute-start(f32[4,128,256]{2,1,0:T(8,128)} %convolution_add_fusion.5), channel_id=1, source_target_pairs={{0,4},{4,8},{8,12},{12,16},{16,20},{20,24},{24,28},{28,32},{32,36}... | collective-permute-start | bytes 1572872 | tf_op jit(solution)/shard_map/while/body/eval_jaxpr/ppermute | solution.py:29
  257.4 10.7 %collective-permute-start = (f32[4,128,256]{2,1,0:T(8,128)}, f32[4,128,256]{2,1,0:T(8,128)S(1)}, u32[]{:S(2)}, u32[]{:S(2)}) collective-permute-start(f32[4,128,256]{2,1,0:T(8,128)} %convolution_add_fusion.5), channel_id=1, source_target_pairs={{0,4},{4,8},{8,12},{12,16},{16,20},{20,24},{24,28},{28,32},{32,36}... | collective-permute-start | bytes 1572872 | tf_op jit(solution)/shard_map/while/body/eval_jaxpr/ppermute | solution.py:29
  270.4 10.7 %collective-permute-start = (f32[4,128,256]{2,1,0:T(8,128)}, f32[4,128,256]{2,1,0:T(8,128)S(1)}, u32[]{:S(2)}, u32[]{:S(2)}) collective-permute-start(f32[4,128,256]{2,1,0:T(8,128)} %convolution_add_fusion.5), channel_id=1, source_target_pairs={{0,4},{4,8},{8,12},{12,16},{16,20},{20,24},{24,28},{28,32},{32,36}... | collective-permute-start | bytes 1572872 | tf_op jit(solution)/shard_map/while/body/eval_jaxpr/ppermute | solution.py:29
  283.4 10.7 %collective-permute-start = (f32[4,128,256]{2,1,0:T(8,128)}, f32[4,128,256]{2,1,0:T(8,128)S(1)}, u32[]{:S(2)}, u32[]{:S(2)}) collective-permute-start(f32[4,128,256]{2,1,0:T(8,128)} %convolution_add_fusion.5), channel_id=1, source_target_pairs={{0,4},{4,8},{8,12},{12,16},{16,20},{20,24},{24,28},{28,32},{32,36}... | collective-permute-start | bytes 1572872 | tf_op jit(solution)/shard_map/while/body/eval_jaxpr/ppermute | solution.py:29
  296.4 10.7 %collective-permute-start = (f32[4,128,256]{2,1,0:T(8,128)}, f32[4,128,256]{2,1,0:T(8,128)S(1)}, u32[]{:S(2)}, u32[]{:S(2)}) collective-permute-start(f32[4,128,256]{2,1,0:T(8,128)} %convolution_add_fusion.5), channel_id=1, source_target_pairs={{0,4},{4,8},{8,12},{12,16},{16,20},{20,24},{24,28},{28,32},{32,36}... | collective-permute-start | bytes 1572872 | tf_op jit(solution)/shard_map/while/body/eval_jaxpr/ppermute | solution.py:29
  309.5 10.7 %collective-permute-start = (f32[4,128,256]{2,1,0:T(8,128)}, f32[4,128,256]{2,1,0:T(8,128)S(1)}, u32[]{:S(2)}, u32[]{:S(2)}) collective-permute-start(f32[4,128,256]{2,1,0:T(8,128)} %convolution_add_fusion.5), channel_id=1, source_target_pairs={{0,4},{4,8},{8,12},{12,16},{16,20},{20,24},{24,28},{28,32},{32,36}... | collective-permute-start | bytes 1572872 | tf_op jit(solution)/shard_map/while/body/eval_jaxpr/ppermute | solution.py:29
  322.5 10.7 %collective-permute-start = (f32[4,128,256]{2,1,0:T(8,128)}, f32[4,128,256]{2,1,0:T(8,128)S(1)}, u32[]{:S(2)}, u32[]{:S(2)}) collective-permute-start(f32[4,128,256]{2,1,0:T(8,128)} %convolution_add_fusion.5), channel_id=1, source_target_pairs={{0,4},{4,8},{8,12},{12,16},{16,20},{20,24},{24,28},{28,32},{32,36}... | collective-permute-start | bytes 1572872 | tf_op jit(solution)/shard_map/while/body/eval_jaxpr/ppermute | solution.py:29
  335.5 10.7 %collective-permute-start = (f32[4,128,256]{2,1,0:T(8,128)}, f32[4,128,256]{2,1,0:T(8,128)S(1)}, u32[]{:S(2)}, u32[]{:S(2)}) collective-permute-start(f32[4,128,256]{2,1,0:T(8,128)} %convolution_add_fusion.5), channel_id=1, source_target_pairs={{0,4},{4,8},{8,12},{12,16},{16,20},{20,24},{24,28},{28,32},{32,36}... | collective-permute-start | bytes 1572872 | tf_op jit(solution)/shard_map/while/body/eval_jaxpr/ppermute | solution.py:29
  348.5 10.7 %collective-permute-start = (f32[4,128,256]{2,1,0:T(8,128)}, f32[4,128,256]{2,1,0:T(8,128)S(1)}, u32[]{:S(2)}, u32[]{:S(2)}) collective-permute-start(f32[4,128,256]{2,1,0:T(8,128)} %convolution_add_fusion.5), channel_id=1, source_target_pairs={{0,4},{4,8},{8,12},{12,16},{16,20},{20,24},{24,28},{28,32},{32,36}... | collective-permute-start | bytes 1572872 | tf_op jit(solution)/shard_map/while/body/eval_jaxpr/ppermute | solution.py:29
  361.6 10.7 %collective-permute-start = (f32[4,128,256]{2,1,0:T(8,128)}, f32[4,128,256]{2,1,0:T(8,128)S(1)}, u32[]{:S(2)}, u32[]{:S(2)}) collective-permute-start(f32[4,128,256]{2,1,0:T(8,128)} %convolution_add_fusion.5), channel_id=1, source_target_pairs={{0,4},{4,8},{8,12},{12,16},{16,20},{20,24},{24,28},{28,32},{32,36}... | collective-permute-start | bytes 1572872 | tf_op jit(solution)/shard_map/while/body/eval_jaxpr/ppermute | solution.py:29
  374.6 10.7 %collective-permute-start = (f32[4,128,256]{2,1,0:T(8,128)}, f32[4,128,256]{2,1,0:T(8,128)S(1)}, u32[]{:S(2)}, u32[]{:S(2)}) collective-permute-start(f32[4,128,256]{2,1,0:T(8,128)} %convolution_add_fusion.5), channel_id=1, source_target_pairs={{0,4},{4,8},{8,12},{12,16},{16,20},{20,24},{24,28},{28,32},{32,36}... | collective-permute-start | bytes 1572872 | tf_op jit(solution)/shard_map/while/body/eval_jaxpr/ppermute | solution.py:29
  387.6 10.7 %collective-permute-start = (f32[4,128,256]{2,1,0:T(8,128)}, f32[4,128,256]{2,1,0:T(8,128)S(1)}, u32[]{:S(2)}, u32[]{:S(2)}) collective-permute-start(f32[4,128,256]{2,1,0:T(8,128)} %convolution_add_fusion.5), channel_id=1, source_target_pairs={{0,4},{4,8},{8,12},{12,16},{16,20},{20,24},{24,28},{28,32},{32,36}... | collective-permute-start | bytes 1572872 | tf_op jit(solution)/shard_map/while/body/eval_jaxpr/ppermute | solution.py:29
  413.7 12.0 %collective-permute-start = (f32[4,128,256]{2,1,0:T(8,128)}, f32[4,128,256]{2,1,0:T(8,128)S(1)}, u32[]{:S(2)}, u32[]{:S(2)}) collective-permute-start(f32[4,128,256]{2,1,0:T(8,128)} %convolution_add_fusion.5), channel_id=1, source_target_pairs={{0,4},{4,8},{8,12},{12,16},{16,20},{20,24},{24,28},{28,32},{32,36}... | collective-permute-start | bytes 1572872 | tf_op jit(solution)/shard_map/while/body/eval_jaxpr/ppermute | solution.py:29
  428.1 12.8 %collective-permute-start = (f32[4,128,256]{2,1,0:T(8,128)}, f32[4,128,256]{2,1,0:T(8,128)S(1)}, u32[]{:S(2)}, u32[]{:S(2)}) collective-permute-start(f32[4,128,256]{2,1,0:T(8,128)} %convolution_add_fusion.5), channel_id=1, source_target_pairs={{0,4},{4,8},{8,12},{12,16},{16,20},{20,24},{24,28},{28,32},{32,36}... | collective-permute-start | bytes 1572872 | tf_op jit(solution)/shard_map/while/body/eval_jaxpr/ppermute | solution.py:29
  443.2 12.8 %collective-permute-start = (f32[4,128,256]{2,1,0:T(8,128)}, f32[4,128,256]{2,1,0:T(8,128)S(1)}, u32[]{:S(2)}, u32[]{:S(2)}) collective-permute-start(f32[4,128,256]{2,1,0:T(8,128)} %convolution_add_fusion.5), channel_id=1, source_target_pairs={{0,4},{4,8},{8,12},{12,16},{16,20},{20,24},{24,28},{28,32},{32,36}... | collective-permute-start | bytes 1572872 | tf_op jit(solution)/shard_map/while/body/eval_jaxpr/ppermute | solution.py:29
  458.3 12.8 %collective-permute-start = (f32[4,128,256]{2,1,0:T(8,128)}, f32[4,128,256]{2,1,0:T(8,128)S(1)}, u32[]{:S(2)}, u32[]{:S(2)}) collective-permute-start(f32[4,128,256]{2,1,0:T(8,128)} %convolution_add_fusion.5), channel_id=1, source_target_pairs={{0,4},{4,8},{8,12},{12,16},{16,20},{20,24},{24,28},{28,32},{32,36}... | collective-permute-start | bytes 1572872 | tf_op jit(solution)/shard_map/while/body/eval_jaxpr/ppermute | solution.py:29
  473.5 12.8 %collective-permute-start = (f32[4,128,256]{2,1,0:T(8,128)}, f32[4,128,256]{2,1,0:T(8,128)S(1)}, u32[]{:S(2)}, u32[]{:S(2)}) collective-permute-start(f32[4,128,256]{2,1,0:T(8,128)} %convolution_add_fusion.5), channel_id=1, source_target_pairs={{0,4},{4,8},{8,12},{12,16},{16,20},{20,24},{24,28},{28,32},{32,36}... | collective-permute-start | bytes 1572872 | tf_op jit(solution)/shard_map/while/body/eval_jaxpr/ppermute | solution.py:29
  488.6 12.8 %collective-permute-start = (f32[4,128,256]{2,1,0:T(8,128)}, f32[4,128,256]{2,1,0:T(8,128)S(1)}, u32[]{:S(2)}, u32[]{:S(2)}) collective-permute-start(f32[4,128,256]{2,1,0:T(8,128)} %convolution_add_fusion.5), channel_id=1, source_target_pairs={{0,4},{4,8},{8,12},{12,16},{16,20},{20,24},{24,28},{28,32},{32,36}... | collective-permute-start | bytes 1572872 | tf_op jit(solution)/shard_map/while/body/eval_jaxpr/ppermute | solution.py:29
  503.7 12.8 %collective-permute-start = (f32[4,128,256]{2,1,0:T(8,128)}, f32[4,128,256]{2,1,0:T(8,128)S(1)}, u32[]{:S(2)}, u32[]{:S(2)}) collective-permute-start(f32[4,128,256]{2,1,0:T(8,128)} %convolution_add_fusion.5), channel_id=1, source_target_pairs={{0,4},{4,8},{8,12},{12,16},{16,20},{20,24},{24,28},{28,32},{32,36}... | collective-permute-start | bytes 1572872 | tf_op jit(solution)/shard_map/while/body/eval_jaxpr/ppermute | solution.py:29
  518.9 12.8 %collective-permute-start = (f32[4,128,256]{2,1,0:T(8,128)}, f32[4,128,256]{2,1,0:T(8,128)S(1)}, u32[]{:S(2)}, u32[]{:S(2)}) collective-permute-start(f32[4,128,256]{2,1,0:T(8,128)} %convolution_add_fusion.5), channel_id=1, source_target_pairs={{0,4},{4,8},{8,12},{12,16},{16,20},{20,24},{24,28},{28,32},{32,36}... | collective-permute-start | bytes 1572872 | tf_op jit(solution)/shard_map/while/body/eval_jaxpr/ppermute | solution.py:29
  534.0 12.8 %collective-permute-start = (f32[4,128,256]{2,1,0:T(8,128)}, f32[4,128,256]{2,1,0:T(8,128)S(1)}, u32[]{:S(2)}, u32[]{:S(2)}) collective-permute-start(f32[4,128,256]{2,1,0:T(8,128)} %convolution_add_fusion.5), channel_id=1, source_target_pairs={{0,4},{4,8},{8,12},{12,16},{16,20},{20,24},{24,28},{28,32},{32,36}... | collective-permute-start | bytes 1572872 | tf_op jit(solution)/shard_map/while/body/eval_jaxpr/ppermute | solution.py:29
  549.1 12.8 %collective-permute-start = (f32[4,128,256]{2,1,0:T(8,128)}, f32[4,128,256]{2,1,0:T(8,128)S(1)}, u32[]{:S(2)}, u32[]{:S(2)}) collective-permute-start(f32[4,128,256]{2,1,0:T(8,128)} %convolution_add_fusion.5), channel_id=1, source_target_pairs={{0,4},{4,8},{8,12},{12,16},{16,20},{20,24},{24,28},{28,32},{32,36}... | collective-permute-start | bytes 1572872 | tf_op jit(solution)/shard_map/while/body/eval_jaxpr/ppermute | solution.py:29
  564.3 12.8 %collective-permute-start = (f32[4,128,256]{2,1,0:T(8,128)}, f32[4,128,256]{2,1,0:T(8,128)S(1)}, u32[]{:S(2)}, u32[]{:S(2)}) collective-permute-start(f32[4,128,256]{2,1,0:T(8,128)} %convolution_add_fusion.5), channel_id=1, source_target_pairs={{0,4},{4,8},{8,12},{12,16},{16,20},{20,24},{24,28},{28,32},{32,36}... | collective-permute-start | bytes 1572872 | tf_op jit(solution)/shard_map/while/body/eval_jaxpr/ppermute | solution.py:29
  579.4 12.8 %collective-permute-start = (f32[4,128,256]{2,1,0:T(8,128)}, f32[4,128,256]{2,1,0:T(8,128)S(1)}, u32[]{:S(2)}, u32[]{:S(2)}) collective-permute-start(f32[4,128,256]{2,1,0:T(8,128)} %convolution_add_fusion.5), channel_id=1, source_target_pairs={{0,4},{4,8},{8,12},{12,16},{16,20},{20,24},{24,28},{28,32},{32,36}... | collective-permute-start | bytes 1572872 | tf_op jit(solution)/shard_map/while/body/eval_jaxpr/ppermute | solution.py:29
  594.6 12.8 %collective-permute-start = (f32[4,128,256]{2,1,0:T(8,128)}, f32[4,128,256]{2,1,0:T(8,128)S(1)}, u32[]{:S(2)}, u32[]{:S(2)}) collective-permute-start(f32[4,128,256]{2,1,0:T(8,128)} %convolution_add_fusion.5), channel_id=1, source_target_pairs={{0,4},{4,8},{8,12},{12,16},{16,20},{20,24},{24,28},{28,32},{32,36}... | collective-permute-start | bytes 1572872 | tf_op jit(solution)/shard_map/while/body/eval_jaxpr/ppermute | solution.py:29
  622.6 39.4 %collective-permute-start.2 = (f32[256,2048]{1,0:T(8,128)}, f32[256,2048]{1,0:T(8,128)S(1)}, u32[]{:S(2)}, u32[]{:S(2)}) collective-permute-start(f32[256,2048]{1,0:T(8,128)} %fusion.47), channel_id=1, source_target_pairs={{0,1},{1,0},{2,3},{3,2},{4,5},{5,4},{6,7},{7,6},{8,9},{9,8},{10,11... | collective-permute-start | bytes 6291464 | tf_op jit(solution)/shard_map/ppermute | solution.py:18
  665.1 45.3 %collective-permute-start.3 = (f32[256,2048]{1,0:T(8,128)}, f32[256,2048]{1,0:T(8,128)}, u32[]{:S(2)}, u32[]{:S(2)}) collective-permute-start(f32[256,2048]{1,0:T(8,128)} %add.210), channel_id=1, source_target_pairs={{0,2},{1,3},{2,0},{3,1},{4,6},{5,7},{6,4},{7,5},{8,10},{9,11},{10,... | collective-permute-start | bytes 6291464 | tf_op jit(solution)/shard_map/ppermute | solution.py:18
  (43 other events, 412.7 us)
